TPU v7x, 32 devices: a whole 2x2x4 slice. The times are simulated.
32 devices in a mesh: parts: 2 (over y), users: 16 (over z, x, core).
Axes of the slice: x: 2, y: 2, z: 4, core: 2. Of those that a mesh axis runs over, the one named last changes fastest.
Arguments:
- candidates: bfloat16 [512, 512], P(('parts', 'users')), parts along dimension 0, may hold values from -6 to 6
- candidate_user: int32 [512], P(('parts', 'users')), parts along dimension 0, may hold values from 0 to 7
- events: bfloat16 [65536, 512], P(('parts', 'users')), parts along dimension 0, may hold values from -6 to 6
- event_user: int32 [65536], P(('parts', 'users')), parts along dimension 0, may hold values from 0 to 7, never falling along the last dimension, each value on 1 to 12288 neighbouring positions
- event_mask: int32 [65536], P(('parts', 'users')), parts along dimension 0, may hold values 0 or 1
- query_weight: bfloat16 [512, 512], replicated, may hold values from -0.25 to 0.25
- key_weight: bfloat16 [512, 512], replicated, may hold values from -0.25 to 0.25
- value_weight: bfloat16 [512, 512], replicated, may hold values from -2 to 2
- gate_weight: bfloat16 [512, 512], replicated, may hold values from -0.25 to 0.25
- output_weight: bfloat16 [512, 512], replicated, may hold values from -0.25 to 0.25
Outputs:
- candidate_out: bfloat16 [512, 512], P(('parts', 'users')), parts along dimension 0
There are 2 independent parts, one for each index of `parts`. A program takes and returns all parts, laid end to end along the dimension named above; an argument that names none is the same for every part. Nothing has to cross between parts.
Inputs may be any that keep to these rules, and one draw needn't show every extreme that they name: event_user never falls along the events; each user's events form one run of at most 12288 slots.
All inputs are finite; a program needn't handle non-finite values. No bound on the sum of `event_mask` on one device may be relied on, other than what follows from the above.
Results may differ from a plain program's by a relative error of at most 0.0044.
Values may be sent and summed in bfloat16 or wider, within the bound.
No kernel may reach another device: no remote copies, remote signals or barrier semaphores. Data moves between devices by JAX's collectives and lax.ppermute only.
A program may use at most 64 MiB of HBM per device.

v0:
```python
import math
import jax
import jax.numpy as jnp
from jax import lax
from jax.sharding import PartitionSpec as P

HEADS = 4


def per_device(
    candidates,
    candidate_user,
    events,
    event_user,
    event_mask,
    query_weight,
    key_weight,
    value_weight,
    gate_weight,
    output_weight,
):
    own_count = candidates.shape[0]
    model_width = candidates.shape[1]
    head_count = HEADS
    head_size = model_width // head_count
    score_scale = 1.0 / math.sqrt(head_size)
    queries = jnp.dot(candidates, query_weight, preferred_element_type=jnp.float32).astype(
        jnp.bfloat16
    )
    gate_values = jax.nn.silu(jnp.dot(candidates, gate_weight, preferred_element_type=jnp.float32))
    key_rows = jnp.dot(events, key_weight, preferred_element_type=jnp.float32).astype(jnp.bfloat16)
    value_rows = jnp.dot(events, value_weight, preferred_element_type=jnp.float32).astype(
        jnp.bfloat16
    )
    event_count = key_rows.shape[0]
    key_heads = key_rows.reshape(event_count, head_count, head_size)
    value_heads = value_rows.reshape(event_count, head_count, head_size)
    valid_events = event_mask.astype(jnp.float32)
    all_queries, all_users = (
        lax.all_gather(queries, "users", axis=0, tiled=True),
        lax.all_gather(candidate_user, "users", axis=0, tiled=True),
    )

    def one_block(block_pair):
        query_block, user_block = block_pair
        scores = (
            jnp.einsum("chd,ehd->hce", query_block, key_heads, preferred_element_type=jnp.float32)
            * score_scale
        )
        same_user = (user_block[:, None] == event_user[None, :]).astype(jnp.float32) * valid_events[
            None, :
        ]
        attn_weights = (jax.nn.silu(scores) * same_user[None]).astype(jnp.bfloat16)
        mixed_rows = jnp.einsum(
            "hce,ehd->chd", attn_weights, value_heads, preferred_element_type=jnp.float32
        )
        return mixed_rows.reshape(query_block.shape[0], model_width)

    row_count = own_count * lax.axis_size("users")
    row_block = math.gcd(row_count, 512)
    query_part = all_queries
    query_part = query_part.reshape(row_count // row_block, row_block, head_count, head_size)
    user_part = all_users.reshape(row_count // row_block, row_block)
    summed = lax.psum_scatter(
        lax.map(one_block, (query_part, user_part)).reshape(row_count, model_width),
        "users",
        scatter_dimension=0,
        tiled=True,
    )
    mean_row = jnp.mean(summed, axis=1, keepdims=True)
    centred = summed - mean_row
    var_row = jnp.mean(centred * centred, axis=1, keepdims=True)
    normed = centred / jnp.sqrt(var_row + 1e-05)
    gated_rows = (normed * gate_values).astype(jnp.bfloat16)
    result = candidates.astype(jnp.float32) + jnp.dot(
        gated_rows, output_weight, preferred_element_type=jnp.float32
    )
    return result.astype(jnp.bfloat16)


def solution(mesh):
    in_specs = (
        P(("parts", "users"), None),
        P(("parts", "users")),
        P(("parts", "users"), None),
        P(("parts", "users")),
        P(("parts", "users")),
        P(),
        P(),
        P(),
        P(),
        P(),
    )
    out_specs = P(("parts", "users"), None)
    return jax.shard_map(
        per_device, mesh=mesh, in_specs=in_specs, out_specs=out_specs, check_vma=False
    )
```

profile of v0, /device:TPU:0, one launch (start us, length us, event | category | flops | bytes accessed | tf_op | source)
XLA Modules:
  0.0 126.6 jit_solution(15532757817765731174)
XLA Ops:
  6.5 0.0 copy-start
  6.5 0.0 reduce-scatter.2.cloned.1.call-start
  6.5 1.4 %dynamic-slice.1 = u32[1]{0:T(128)} dynamic-slice(u32[32]{0:T(128)} %constant.34, u32[]{:T(128)S(6)} %add.28), dynamic_slice_sizes={1} | dynamic-slice | bytes 12
  8.6 0.9 dynamic-update-slice
  9.4 13.7 %all-reduce = s32[256]{0:T(256)S(1)} all-reduce(s32[256]{0:T(256)S(1)} %dynamic-update-slice), channel_id=1, replica_groups=mesh['parts'=2,'users'=16] {'users'}, use_global_device_ids=true, to_apply=%add | all-reduce | flops 256 | bytes 2048
  23.2 0.7 convert_element_type.31
  23.9 1.2 convolution_convert_fusion.2
  25.1 18.7 %all_gather.6 = bf16[256,512]{1,0:T(8,128)(2,1)S(1)} all-gather(bf16[16,512]{1,0:T(8,128)(2,1)S(1)} %convolution_convert_fusion.2), channel_id=1, replica_groups=mesh['parts'=2,'users'=16] {'users'}, dimensions={0}, use_global_device_ids=true | all-gather | bytes 278528 | tf_op jit(solution)/shard_map/all_gather | solution.py:40
  43.8 0.0 copy-done
  43.8 0.0 copy-start.5
  43.8 3.7 %convolution_convert_fusion = bf16[2048,512]{0,1:T(8,128)(2,1)} fusion(bf16[2048,512]{1,0:T(8,128)(2,1)S(1)} %copy-done, bf16[512,512]{1,0:T(8,128)(2,1)} %param.16), kind=kOutput, calls=%fused_computation.1 | convolution fusion | flops 1074790400 | bytes 4718592 | tf_op jit(solution)/shard_map/dot_general | solution.py:31
  47.5 0.0 copy-done.5
  47.5 0.0 copy-start.4
  47.5 2.7 %convolution_convert_fusion.1 = bf16[2048,512]{0,1:T(8,128)(2,1)} fusion(bf16[2048,512]{1,0:T(8,128)(2,1)S(1)} %copy-done, bf16[512,512]{1,0:T(8,128)(2,1)S(1)} %copy-done.5), kind=kOutput, calls=%fused_computation.2 | convolution fusion | flops 1074790400 | bytes 4718592 | tf_op jit(solution)/shard_map/dot_general | solution.py:32
  50.1 0.0 copy-done.4
  50.1 1.5 %compare_select_fusion = f32[256,2048]{1,0:T(8,128)} fusion(f32[2048]{0:T(1024)S(1)} %convert_element_type.31, s32[2048]{0:T(1024)S(1)} %copy-done.4, s32[256]{0:T(256)S(1)} %all-reduce), kind=kLoop, calls=%fused_computation.3 | loop fusion | flops 1048576 | bytes 2114560 | tf_op jit(solution)/shard_map/while/body/eval_jaxpr/mul | solution.py:50
  51.7 0.0 copy-start.1
  51.7 0.0 copy-start.2
  51.7 0.0 copy-start.3
  51.7 8.2 %fusion = f32[4,128,256]{2,1,0:T(8,128)} fusion(bf16[2048,4,128]{0,2,1:T(8,128)(2,1)} %bitcast.28, bf16[2048,4,128]{0,2,1:T(8,128)(2,1)} %bitcast.27, f32[256,2048]{1,0:T(8,128)} %compare_select_fusion, bf16[256,512]{1,0:T(8,128)(2,1)S(1)} %all_gather.6), kind=kOutput, calls=%fused_computation.4 | convolution fusion | flops 1088421888 | bytes 7077888 | tf_op jit(solution)/shard_map/while/body/eval_jaxpr/hce,ehd->chd/dot_general | solution.py:54
  59.9 2.0 %copy.13 = f32[256,512]{1,0:T(8,128)} copy(f32[256,512]{0,1:T(8,128)} %bitcast.26) | data formatting | bytes 1048576 | tf_op jit(solution)/shard_map/reshape | solution.py:65
  61.9 0.0 reduce-scatter.2.cloned.1.call-update
  61.9 54.3 %reduce-scatter.2.cloned.1.call-done = f32[16,512]{1,0:T(8,128)} async-done(((f32[256,512]{1,0:T(8,128)}), f32[16,512]{1,0:T(8,128)}) %reduce-scatter.2.cloned.1.call-update) | async-done | bytes 32784 | tf_op jit(solution)/shard_map/reduce_scatter | solution.py:64
  116.2 0.9 reduce_sum.18
  117.1 0.9 multiply_reduce_fusion
  118.0 0.0 copy-done.1
  118.0 0.0 copy-done.2
  118.1 0.0 copy-done.3
  118.1 1.7 %fusion.1 = bf16[16,512]{1,0:T(8,128)(2,1)} fusion(bf16[512,512]{1,0:T(8,128)(2,1)S(1)} %copy-done.1, bf16[16,512]{1,0:T(8,128)(2,1)S(1)} %copy-done.3, f32[16,512]{1,0:T(8,128)} %reduce-scatter.2.cloned.1.call-done, f32[16]{0:T(128)S(1)} %add_sqrt_fusion, f32[16]{0:T(128)S(1)} %broadcast_multiply_fusion, bf16[512,512]{1,0:T(8,128)(2,1)S(1)} %copy-done.2), kind=kOutput, calls=%fused_computation.6 | convolution fusion | flops 16867328 | bytes 1114240 | tf_op jit(solution)/shard_map/dot_general | solution.py:75
  (3 shorter events, 0.0 us)
Async XLA Ops:
  6.5 37.2 %copy-start = (bf16[2048,512]{1,0:T(8,128)(2,1)S(1)}, bf16[2048,512]{1,0:T(8,128)(2,1)}, u32[]{:S(2)}) copy-start(bf16[2048,512]{1,0:T(8,128)(2,1)} %param.12) | copy-start | bytes 6291460
  6.5 109.7 %reduce-scatter.2.cloned.1.call-start = ((), (), s32[]{:S(2)}) async-start(), calls=%async_computation.1 | async-start | bytes 557056 | tf_op jit(solution)/shard_map/reduce_scatter | solution.py:64
  43.8 3.7 %copy-start.5 = (bf16[512,512]{1,0:T(8,128)(2,1)S(1)}, bf16[512,512]{1,0:T(8,128)(2,1)}, u32[]{:S(2)}) copy-start(bf16[512,512]{1,0:T(8,128)(2,1)} %param.17) | copy-start | bytes 1572868
  47.5 2.7 %copy-start.4 = (s32[2048]{0:T(1024)S(1)}, s32[2048]{0:T(1024)}, u32[]{:S(2)}) copy-start(s32[2048]{0:T(1024)} %param.13) | copy-start | bytes 24580
  51.7 66.4 %copy-start.1 = (bf16[512,512]{1,0:T(8,128)(2,1)S(1)}, bf16[512,512]{1,0:T(8,128)(2,1)}, u32[]{:S(2)}) copy-start(bf16[512,512]{1,0:T(8,128)(2,1)} %param.19) | copy-start | bytes 1572868
  51.7 66.4 %copy-start.2 = (bf16[512,512]{1,0:T(8,128)(2,1)S(1)}, bf16[512,512]{1,0:T(8,128)(2,1)}, u32[]{:S(2)}) copy-start(bf16[512,512]{1,0:T(8,128)(2,1)} %param.18) | copy-start | bytes 1572868
  51.7 66.4 %copy-start.3 = (bf16[16,512]{1,0:T(8,128)(2,1)S(1)}, bf16[16,512]{1,0:T(8,128)(2,1)}, u32[]{:S(2)}) copy-start(bf16[16,512]{1,0:T(8,128)(2,1)} %param.10) | copy-start | bytes 49156
Sparse Core Ops, SparseCore 0:
  62.0 54.1 reduce-scatter.1
where the time goes:
time: 127 us
  waiting for transfers between devices  54.3 us (43%)
  blocking collectives  32.4 us (26%)
  matrix products  17.5 us (14%)
  between operations  14.1 us (11%)
  local copies, waits for them, and re-layouts  4.3 us (3%)
  other arithmetic  4.07 us (3%)
    reduce_scatter x1, waiting for transfers between devices, per_device(): lax.psum_scatter(lax.map(one_block, (query_part, user_part)).reshape(row_...  54.3 us
    all_gather x1, blocking collectives, per_device(): lax.all_gather(queries, 'users', axis=0, tiled=True)  18.7 us
    unnamed x1, blocking collectives  13.7 us
    dot_general x1, matrix products, one_block(): jnp.einsum('hce,ehd->chd', attn_weights, value_heads, preferred_element_t...  8.19 us
    dot_general x1, matrix products, per_device(): jnp.dot(events, key_weight, preferred_element_type=jnp.float32)  3.69 us
    dot_general x1, matrix products, per_device(): jnp.dot(events, value_weight, preferred_element_type=jnp.float32)  2.65 us
  transfers between devices with their start and end apart: 1, of which 1 were waited for; matrix products, arithmetic and copies ran while one was open for 0% of the time, Pallas kernels for 0%

commit v1 on v0

--- a/solution.py
+++ b/solution.py
@@ -36,8 +36,15 @@
     key_heads = key_rows.reshape(event_count, head_count, head_size)
     value_heads = value_rows.reshape(event_count, head_count, head_size)
     valid_events = event_mask.astype(jnp.float32)
+
+    def watch_the_meshes(z_in, dim_k):
+        state_next = lax.axis_size("users")
+        val2 = jnp.stack([z_in] * state_next)
+        carry = lax.all_to_all(val2, "users", 0, 0)
+        return jnp.concatenate(carry, dim_k)
+
     all_queries, all_users = (
-        lax.all_gather(queries, "users", axis=0, tiled=True),
+        watch_the_meshes(queries, 0),
         lax.all_gather(candidate_user, "users", axis=0, tiled=True),
     )
 

time: 127 us -> 115 us (0.906)
  blocking collectives: 32.4 us -> 12.4 us
  starting transfers between devices: 0.01 us -> 7.43 us
    all_gather x1 -> x0, blocking collectives: 18.7 us -> none  [per_device(): lax.all_gather(queries, 'users', axis=0, tiled=True)]
    all_to_all x0 -> x1, starting transfers between devices: none -> 7.39 us  [watch_the_meshes(): carry = lax.all_to_all(val2, 'users', 0, 0)]
    unnamed x1, blocking collectives: 13.7 us -> 12.4 us
  transfers between devices with their start and end apart: 1 -> 2, of which waited for: 1 -> 1; matrix products, arithmetic and copies ran while one was open for 0% -> 9% of each run, Pallas kernels for 0% -> 0%
where the time goes in v1:
time: 115 us
  waiting for transfers between devices  53.9 us (47%)
  matrix products  17.7 us (15%)
  between operations  14.1 us (12%)
  blocking collectives  12.4 us (11%)
  starting transfers between devices  7.43 us (6%)
  local copies, waits for them, and re-layouts  4.98 us (4%)
  other arithmetic  4.07 us (4%)
    reduce_scatter x1, waiting for transfers between devices, per_device(): lax.psum_scatter(lax.map(one_block, (query_part, user_part)).reshape(row_...  53.9 us
    unnamed x1, blocking collectives  12.4 us
    dot_general x1, matrix products, one_block(): jnp.einsum('hce,ehd->chd', attn_weights, value_heads, preferred_element_t...  8.25 us
    all_to_all x1, starting transfers between devices, watch_the_meshes(): carry = lax.all_to_all(val2, 'users', 0, 0)  7.39 us
    dot_general x1, matrix products, per_device(): jnp.dot(events, key_weight, preferred_element_type=jnp.float32)  3.69 us
    dot_general x1, matrix products, per_device(): jnp.dot(events, value_weight, preferred_element_type=jnp.float32)  2.65 us
  transfers between devices with their start and end apart: 2, of which 1 were waited for; matrix products, arithmetic and copies ran while one was open for 9% of the time, Pallas kernels for 0%

profile of v1, /device:TPU:0, one launch (start us, length us, event | category | flops | bytes accessed | tf_op | source)
XLA Modules:
  0.0 114.6 jit_solution(9066931620304522641)
XLA Ops:
  6.5 0.0 copy-start
  6.5 1.4 %convolution_convert_fusion.2 = bf16[16,512]{1,0:T(8,128)(2,1)S(1)} fusion(bf16[16,512]{1,0:T(8,128)(2,1)} %param.10, bf16[512,512]{1,0:T(8,128)(2,1)} %param.15), kind=kOutput, calls=%fused_computation.7 | convolution fusion | flops 8396800 | bytes 557056 | tf_op jit(solution)/shard_map/dot_general | solution.py:27
  7.9 0.8 stack.2
  8.7 7.4 %all-to-all-start = ((bf16[16,16,512]{2,1,0:T(8,128)(2,1)}), bf16[16,16,512]{2,1,0:T(8,128)(2,1)S(1)}, u32[]{:S(2)}, u32[]{:S(2)}) async-start(bf16[16,16,512]{2,1,0:T(8,128)(2,1)} %stack.2), calls=%async_computation | async-start | bytes 524288 | tf_op jit(solution)/shard_map/all_to_all | solution.py:43
  16.1 0.0 reduce-scatter.2.cloned.1.call-start
  16.1 1.2 %dynamic-slice.1 = u32[1]{0:T(128)} dynamic-slice(u32[32]{0:T(128)} %constant.34, u32[]{:T(128)S(6)} %add.28), dynamic_slice_sizes={1} | dynamic-slice | bytes 12
  18.0 0.9 dynamic-update-slice
  18.9 12.4 %all-reduce = s32[256]{0:T(256)S(1)} all-reduce(s32[256]{0:T(256)S(1)} %dynamic-update-slice), channel_id=1, replica_groups=mesh['parts'=2,'users'=16] {'users'}, use_global_device_ids=true, to_apply=%add | all-reduce | flops 256 | bytes 2048
  31.3 0.7 convert_element_type.31
  32.0 0.0 copy-done
  32.0 0.0 copy-start.5
  32.0 3.7 %convolution_convert_fusion = bf16[2048,512]{0,1:T(8,128)(2,1)} fusion(bf16[2048,512]{1,0:T(8,128)(2,1)S(1)} %copy-done, bf16[512,512]{1,0:T(8,128)(2,1)} %param.16), kind=kOutput, calls=%fused_computation.1 | convolution fusion | flops 1074790400 | bytes 4718592 | tf_op jit(solution)/shard_map/dot_general | solution.py:31
  35.7 0.0 copy-done.5
  35.7 0.0 copy-start.4
  35.7 2.7 %convolution_convert_fusion.1 = bf16[2048,512]{0,1:T(8,128)(2,1)} fusion(bf16[2048,512]{1,0:T(8,128)(2,1)S(1)} %copy-done, bf16[512,512]{1,0:T(8,128)(2,1)S(1)} %copy-done.5), kind=kOutput, calls=%fused_computation.2 | convolution fusion | flops 1074790400 | bytes 4718592 | tf_op jit(solution)/shard_map/dot_general | solution.py:32
  38.4 0.0 copy-done.4
  38.4 1.5 %compare_select_fusion = f32[256,2048]{1,0:T(8,128)} fusion(f32[2048]{0:T(1024)S(1)} %convert_element_type.31, s32[2048]{0:T(1024)S(1)} %copy-done.4, s32[256]{0:T(256)S(1)} %all-reduce), kind=kLoop, calls=%fused_computation.3 | loop fusion | flops 1048576 | bytes 2114560 | tf_op jit(solution)/shard_map/while/body/eval_jaxpr/mul | solution.py:57
  39.9 0.0 all-to-all-done
  39.9 0.1 squeeze.8
  40.0 0.0 copy-start.1
  40.0 0.0 copy-start.2
  40.0 0.0 copy-start.3
  40.0 8.2 %fusion = f32[4,128,256]{2,1,0:T(8,128)} fusion(bf16[2048,4,128]{0,2,1:T(8,128)(2,1)} %bitcast.19, bf16[2048,4,128]{0,2,1:T(8,128)(2,1)} %bitcast.18, f32[256,2048]{1,0:T(8,128)} %compare_select_fusion, bf16[256,4,128]{2,1,0:T(4,128)(2,1)S(1)} %squeeze.8), kind=kOutput, calls=%fused_computation.4 | convolution fusion | flops 1088421888 | bytes 7077888 | tf_op jit(solution)/shard_map/while/body/eval_jaxpr/hce,ehd->chd/dot_general | solution.py:61
  48.3 2.0 %copy.15 = f32[256,512]{1,0:T(8,128)} copy(f32[256,512]{0,1:T(8,128)} %bitcast.17) | data formatting | bytes 1048576 | tf_op jit(solution)/shard_map/reshape | solution.py:72
  50.3 0.0 reduce-scatter.2.cloned.1.call-update
  50.3 53.9 %reduce-scatter.2.cloned.1.call-done = f32[16,512]{1,0:T(8,128)} async-done(((f32[256,512]{1,0:T(8,128)}), f32[16,512]{1,0:T(8,128)}) %reduce-scatter.2.cloned.1.call-update) | async-done | bytes 32784 | tf_op jit(solution)/shard_map/reduce_scatter | solution.py:71
  104.2 0.9 reduce_sum.18
  105.1 0.9 multiply_reduce_fusion
  106.0 0.0 copy-done.1
  106.0 0.0 copy-done.2
  106.0 0.0 copy-done.3
  106.0 1.7 %fusion.1 = bf16[16,512]{1,0:T(8,128)(2,1)} fusion(bf16[512,512]{1,0:T(8,128)(2,1)S(1)} %copy-done.1, bf16[16,512]{1,0:T(8,128)(2,1)S(1)} %copy-done.3, f32[16,512]{1,0:T(8,128)} %reduce-scatter.2.cloned.1.call-done, f32[16]{0:T(128)S(1)} %add_sqrt_fusion, f32[16]{0:T(128)S(1)} %broadcast_multiply_fusion, bf16[512,512]{1,0:T(8,128)(2,1)S(1)} %copy-done.2), kind=kOutput, calls=%fused_computation.6 | convolution fusion | flops 16867328 | bytes 1114240 | tf_op jit(solution)/shard_map/dot_general | solution.py:82
  (3 shorter events, 0.0 us)
Async XLA Ops:
  6.5 25.5 %copy-start = (bf16[2048,512]{1,0:T(8,128)(2,1)S(1)}, bf16[2048,512]{1,0:T(8,128)(2,1)}, u32[]{:S(2)}) copy-start(bf16[2048,512]{1,0:T(8,128)(2,1)} %param.12) | copy-start | bytes 6291460
  8.7 31.2 %all-to-all-start = ((bf16[16,16,512]{2,1,0:T(8,128)(2,1)}), bf16[16,16,512]{2,1,0:T(8,128)(2,1)S(1)}, u32[]{:S(2)}, u32[]{:S(2)}) async-start(bf16[16,16,512]{2,1,0:T(8,128)(2,1)} %stack.2), calls=%async_computation | async-start | bytes 524288 | tf_op jit(solution)/shard_map/all_to_all | solution.py:43
  16.1 88.1 %reduce-scatter.2.cloned.1.call-start = ((), (), s32[]{:S(2)}) async-start(), calls=%async_computation.2 | async-start | bytes 557056 | tf_op jit(solution)/shard_map/reduce_scatter | solution.py:71
  32.0 3.7 %copy-start.5 = (bf16[512,512]{1,0:T(8,128)(2,1)S(1)}, bf16[512,512]{1,0:T(8,128)(2,1)}, u32[]{:S(2)}) copy-start(bf16[512,512]{1,0:T(8,128)(2,1)} %param.17) | copy-start | bytes 1572868
  35.7 2.7 %copy-start.4 = (s32[2048]{0:T(1024)S(1)}, s32[2048]{0:T(1024)}, u32[]{:S(2)}) copy-start(s32[2048]{0:T(1024)} %param.13) | copy-start | bytes 24580
  40.0 66.0 %copy-start.1 = (bf16[512,512]{1,0:T(8,128)(2,1)S(1)}, bf16[512,512]{1,0:T(8,128)(2,1)}, u32[]{:S(2)}) copy-start(bf16[512,512]{1,0:T(8,128)(2,1)} %param.19) | copy-start | bytes 1572868
  40.0 66.0 %copy-start.2 = (bf16[512,512]{1,0:T(8,128)(2,1)S(1)}, bf16[512,512]{1,0:T(8,128)(2,1)}, u32[]{:S(2)}) copy-start(bf16[512,512]{1,0:T(8,128)(2,1)} %param.18) | copy-start | bytes 1572868
  40.0 66.0 %copy-start.3 = (bf16[16,512]{1,0:T(8,128)(2,1)S(1)}, bf16[16,512]{1,0:T(8,128)(2,1)}, u32[]{:S(2)}) copy-start(bf16[16,512]{1,0:T(8,128)(2,1)} %param.10) | copy-start | bytes 49156
Sparse Core Ops, SparseCore 0:
  50.4 53.7 reduce-scatter.1
